TPU v7x, 256 devices: a whole 4x4x8 slice. The times are simulated.
256 devices in a mesh: ray: 16 (over y, z_lo), pix: 16 (over z_hi, x, core).
Axes of the slice: x: 4, y: 4, z: 8 (z_hi: 2, z_lo: 4; z = z_hi * 4 + z_lo), core: 2. Of those that a mesh axis runs over, the one named last changes fastest.
Arguments:
- positions: float32 [2, 16384], P(None, 'ray'), may hold values from -2 to 2
- directions: float32 [2, 16384], P(None, 'ray'), may hold values from -0.35 to 0.35
- path: float32 [16384], P('ray'), may hold values from -9 to 9
- amplitude: float32 [16384], P('ray'), may hold values from 0.3 to 3
- psf_grad: float32 [3, 1024, 1024], P(None, 'pix', 'ray'), may hold values from -0.3 to 0.3
Outputs:
- psf: float32 [3, 1024, 1024], P(None, 'pix', 'ray')
- ray_grad: float32 [6, 16384], P(None, 'ray')
All inputs are finite; a program needn't handle non-finite values.
Results may differ from a plain program's by a relative error of at most 0.0054.
Values may be sent and summed in bfloat16 or wider, within the bound.
A program may use at most 192 MiB of HBM per device.

v0:
```python
import math
import jax
import jax.numpy as jnp
from jax import lax
from jax.sharding import PartitionSpec as P

NPIX = 1024
wave_scales = (1.2088, 1.0, 0.8953)
two_pi = 2.0 * math.pi


def centred(start, count):
    return (start + jnp.arange(count)).astype(jnp.float32) - 0.5 * NPIX + 0.5


def build_tables(rays, rows_x, cols_y, norm):
    row_list = []
    col_list = []
    weight = (rays[5] * norm)[:, None]
    for wave in range(3):
        scale = wave_scales[wave]
        angle = scale * (
            rays[4][:, None]
            + two_pi
            * (
                rays[2][:, None] * (rows_x[None, :] - rays[0][:, None])
                - rays[3][:, None] * rays[1][:, None]
            )
        )
        row_list.append(jnp.stack([weight * jnp.cos(angle), weight * jnp.sin(angle)]))
        beta = scale * two_pi * cols_y[:, None] * rays[3][None, :]
        col_list.append(jnp.stack([jnp.cos(beta), jnp.sin(beta)]))
    return (jnp.stack(row_list), jnp.stack(col_list))


def mixing(a_re, a_im):
    upper = jnp.concatenate([a_re, a_im], axis=1)
    lower = jnp.concatenate([-a_im, a_re], axis=1)
    return jnp.concatenate([upper, lower], axis=0).astype(jnp.bfloat16)


def product(left, right, dims):
    return lax.dot_general(left, right, dims, preferred_element_type=jnp.float32)


def block_count(count):
    return max(1, min(16, count // 256))


def field_terms(row_tab, col_tab):
    count = row_tab.shape[2]
    nblk = block_count(count)
    blk = count // nblk

    def step(index, total):
        a_blk = lax.dynamic_slice_in_dim(row_tab, index * blk, blk, 2)
        b_blk = lax.dynamic_slice_in_dim(col_tab, index * blk, blk, 3)
        parts = []
        for wave in range(3):
            left = jnp.concatenate([b_blk[wave, 0], b_blk[wave, 1]], axis=1).astype(jnp.bfloat16)
            parts.append(
                product(left, mixing(a_blk[wave, 0], a_blk[wave, 1]), (((1,), (0,)), ((), ())))
            )
        return total + jnp.concatenate(parts, axis=1)

    init = jnp.zeros((col_tab.shape[2], 6 * row_tab.shape[3]), jnp.float32)
    return lax.fori_loop(0, nblk, step, init)


def ray_partials(row_tab, col_tab, rows_x, cols_y, cotangent):
    count = row_tab.shape[2]
    nblk = block_count(count)
    blk = count // nblk
    plen = rows_x.shape[0]

    def one_block(index):
        a_blk = lax.dynamic_slice_in_dim(row_tab, index * blk, blk, 2)
        b_blk = lax.dynamic_slice_in_dim(col_tab, index * blk, blk, 3)
        first = jnp.zeros((blk,), jnp.float32)
        second = jnp.zeros((blk,), jnp.float32)
        third = jnp.zeros((blk,), jnp.float32)
        fourth = jnp.zeros((blk,), jnp.float32)
        for wave in range(3):
            scale = wave_scales[wave]
            a_re = a_blk[wave, 0]
            a_im = a_blk[wave, 1]
            b_re = b_blk[wave, 0]
            b_im = b_blk[wave, 1]
            left = jnp.concatenate([b_re, b_im], axis=1).astype(jnp.bfloat16)
            mix = mixing(a_re, a_im)
            grad_u = cotangent[:, 2 * plen * wave : 2 * plen * (wave + 1)]
            proj = product(left, grad_u, (((0,), (0,)), ((), ())))
            d_are = proj[:blk, :plen] + proj[blk:, plen:]
            d_aim = proj[:blk, plen:] - proj[blk:, :plen]
            d_b = product(grad_u, mix, (((1,), (1,)), ((), ())))
            d_beta = d_b[:, blk:] * b_re - d_b[:, :blk] * b_im
            d_alpha = d_aim * a_re - d_are * a_im
            first = first + scale * jnp.sum(d_alpha, axis=1)
            second = second + scale * two_pi * jnp.sum(d_alpha * rows_x[None, :], axis=1)
            third = third + scale * two_pi * jnp.sum(d_beta * cols_y[:, None], axis=0)
            fourth = fourth + jnp.sum(d_are * a_re + d_aim * a_im, axis=1)
        return jnp.stack([first, second, third, fourth])

    out = lax.map(one_block, jnp.arange(nblk))
    return jnp.transpose(out, (1, 0, 2)).reshape(4, count)


def finish(sums, rays):
    return jnp.stack(
        [
            sums[0],
            -two_pi * rays[2] * sums[0],
            -two_pi * rays[3] * sums[0],
            (sums[1] - two_pi * rays[0] * sums[0]) / NPIX,
            (sums[2] - two_pi * rays[1] * sums[0]) / NPIX,
            sums[3] / rays[5],
        ]
    )


def intensity(field, psf_grad, clen, plen):
    shaped = field.reshape(clen, 3, 2, plen)
    psf = jnp.transpose(shaped[:, :, 0] ** 2 + shaped[:, :, 1] ** 2, (1, 2, 0))
    weight = jnp.transpose(psf_grad, (2, 0, 1))
    grad_u = (2.0 * weight[:, :, None, :] * shaped).reshape(clen, 6 * plen).astype(jnp.bfloat16)
    return (psf, grad_u)


def on_device(positions, directions, path, amplitude, psf_grad):
    rays = jnp.concatenate([positions, directions, path[None], amplitude[None]], axis=0)
    local = rays.shape[1]
    plen = NPIX // lax.axis_size("pix")
    clen = NPIX // lax.axis_size("ray")
    norm = 1.0 / math.sqrt(local * lax.axis_size("ray"))
    rows_x = centred(lax.axis_index("pix") * plen, plen)
    all_cols = centred(0, NPIX)
    row_tab, col_tab = build_tables(rays, rows_x, all_cols, norm)
    field = lax.psum_scatter(field_terms(row_tab, col_tab), "ray", scatter_dimension=0, tiled=True)
    psf, grad_u = intensity(field, psf_grad, clen, plen)
    gathered = lax.all_gather(grad_u, "ray", axis=0, tiled=True)
    partial_value = ray_partials(row_tab, col_tab, rows_x, all_cols, gathered)
    sums = lax.psum(partial_value, "pix")
    return (psf, finish(sums, rays))


def solution(mesh):
    in_specs = (P(None, "ray"), P(None, "ray"), P("ray"), P("ray"), P(None, "pix", "ray"))
    out_specs = (P(None, "pix", "ray"), P(None, "ray"))
    return jax.shard_map(
        on_device, mesh=mesh, in_specs=in_specs, out_specs=out_specs, check_vma=False
    )
```

profile of v0, /device:TPU:32, one launch (start us, length us, event | category | flops | bytes accessed | tf_op | source)
XLA Modules:
  0.0 497.8 jit_solution(16539537502296417018)
XLA Ops:
  9.5 3.6 cosine_multiply_fusion.2
  13.2 46.6 %multiply_cosine_fusion.2 = (f32[1,1024,1024]{2,1,0:T(8,128)}, f32[1,1024,1024]{2,1,0:T(8,128)}, f32[1,1024,1024]{2,1,0:T(8,128)}, f32[1,1024,1024]{2,1,0:T(8,12...) fusion(f32[1024]{0:T(1024)S(1)} %bitcast.214, f32[1024]{0:T(1024)S(1)} %fusion.111, ...), kind=kLoop, calls=%fused_computation.186 | loop fusion | flops 3145728 | bytes 25182208 | tf_op jit(solution)/shard_map/cos | solution.py:32
  62.8 9.3 %maximum_bitcast_fusion.1 = (f32[1,2,1024,1024]{3,2,1,0:T(8,128)S(1)}, f32[1,2,1024,1024]{3,2,1,0:T(8,128)}) fusion(f32[1,1024,1024]{2,1,0:T(8,128)} %get-tuple-element.336, f32[1,1024,1024]{2,1,0:T(8,128)} %get-tuple-element.335, f32[1,1024,1024]{2,1,0:T(8,128)} %get-tuple-element.341, f32[1,1024,1024]{2,1,0:T(8,128)} %get-tuple-element.342), kind=kLoop, calls=%fused_computation.178 | loop fusion | flops 4194304 | bytes 33554432 | tf_op jit(solution)/shard_map/stack | solution.py:33
  72.1 15.7 %fusion.115 = (bf16[3,2,1024,1024]{3,2,1,0:T(8,128)(2,1)}, f32[3,2,1024,1024]{3,2,1,0:T(8,128)}) fusion(f32[1,2,1024,1024]{3,2,1,0:T(8,128)S(1)} %maximum_bitcast_fusion.3, f32[1,2,1024,1024]{3,2,1,0:T(8,128)} %get-tuple-element.346, f32[1,2,1024,1024]{3,2,1,0:T(8,128)S(1)} %get-tuple-element.345), kind=kLoop, calls=%fused_computation.219 | loop fusion | flops 18874368 | bytes 62914560
  87.8 56.3 %while.27 = (s32[]{:T(128)}, f32[1024,384]{0,1:T(8,128)S(1)}, bf16[3,2,1024,1024]{3,2,1,0:T(8,128)(2,1)}, f32[3,2,1024,64]{2,3,1,0:T(8,128)}, s32[]{:T(128)}, /*...) while((s32[]{:T(128)}, f32[1024,384]{0,1:T(8,128)S(1)}, bf16[3,2,1024,1024]{3,2,1,0:T(8,128)(2,1)}, ...), condition=%wide.region_1.0_spmd.clone, body=%wide.region_0.0_spmd.clone.sunk | while | flops 412237824 | bytes 23888080 | solution.py:67
  96.0 2.5 fusion.173
  110.1 2.5 fusion.173
  124.2 2.5 fusion.173
  138.2 2.5 fusion.173
  145.9 87.3 %reduce-scatter.4.cloned.1.call-done = f32[64,384]{1,0:T(8,128)} async-done(((f32[1024,384]{1,0:T(8,128)}), f32[64,384]{1,0:T(8,128)}) %reduce-scatter.4.cloned.1.call-update) | async-done | bytes 98320
  234.4 51.1 %all_gather.3 = bf16[1024,384]{1,0:T(8,128)(2,1)} all-gather(bf16[64,384]{1,0:T(8,128)(2,1)S(1)} %copy.31), channel_id=1, replica_groups=mesh['ray'=16,'pix'=16] {'ray'}, dimensions={0}, use_global_device_ids=true | all-gather | bytes 835584 | tf_op jit(solution)/shard_map/all_gather | solution.py:140
  285.5 118.7 %while.26 = (s32[]{:T(128)}, f32[4,4,256]{2,1,0:T(4,128)S(1)}, s32[4]{0:T(128)S(1)}, f32[3,2,1024,1024]{3,2,1,0:T(8,128)}, bf16[1024,384]{1,0:T(8,128)(2,1)}, /*...) while((s32[]{:T(128)}, f32[4,4,256]{2,1,0:T(4,128)S(1)}, ...), condition=%wide.region_16.17_spmd.clone.clone, body=%wide.region_3.16_spmd.clone.clone.sunk | while | flops 819468480 | bytes 79344528 | solution.py:104
  286.7 5.2 %constant_dynamic-slice_fusion.15 = (f32[1,1,1024,256]{3,2,1,0:T(8,128)S(1)}, f32[1,1,1024,256]{3,2,1,0:T(8,128)}, f32[1,1,1024,256]{3,2,1,0:T(8,128)}, f32[1,1,...) fusion(f32[3,2,1024,1024]{3,2,1,0:T(8,128)} %get-tuple-element.584, ...), kind=kLoop, calls=%fused_computation.102.clone.1 | loop fusion | bytes 12582924 | tf_op jit(solution)/shard_map/while/body/eval_jaxpr/slice | solution.py:87
  295.7 2.5 copy.70
  301.8 2.5 copy.67
  304.3 2.5 copy.68
  316.4 5.2 %constant_dynamic-slice_fusion.15 = (f32[1,1,1024,256]{3,2,1,0:T(8,128)S(1)}, f32[1,1,1024,256]{3,2,1,0:T(8,128)}, f32[1,1,1024,256]{3,2,1,0:T(8,128)}, f32[1,1,...) fusion(f32[3,2,1024,1024]{3,2,1,0:T(8,128)} %get-tuple-element.584, ...), kind=kLoop, calls=%fused_computation.102.clone.1 | loop fusion | bytes 12582924 | tf_op jit(solution)/shard_map/while/body/eval_jaxpr/slice | solution.py:87
  325.4 2.5 copy.70
  329.3 2.1 fusion.160
  331.5 2.5 copy.67
  334.0 2.5 copy.68
  346.1 5.2 %constant_dynamic-slice_fusion.15 = (f32[1,1,1024,256]{3,2,1,0:T(8,128)S(1)}, f32[1,1,1024,256]{3,2,1,0:T(8,128)}, f32[1,1,1024,256]{3,2,1,0:T(8,128)}, f32[1,1,...) fusion(f32[3,2,1024,1024]{3,2,1,0:T(8,128)} %get-tuple-element.584, ...), kind=kLoop, calls=%fused_computation.102.clone.1 | loop fusion | bytes 12582924 | tf_op jit(solution)/shard_map/while/body/eval_jaxpr/slice | solution.py:87
  355.1 2.5 copy.70
  359.0 2.1 fusion.160
  361.1 2.5 copy.67
  363.7 2.5 copy.68
  375.8 5.2 %constant_dynamic-slice_fusion.15 = (f32[1,1,1024,256]{3,2,1,0:T(8,128)S(1)}, f32[1,1,1024,256]{3,2,1,0:T(8,128)}, f32[1,1,1024,256]{3,2,1,0:T(8,128)}, f32[1,1,...) fusion(f32[3,2,1024,1024]{3,2,1,0:T(8,128)} %get-tuple-element.584, ...), kind=kLoop, calls=%fused_computation.102.clone.1 | loop fusion | bytes 12582924 | tf_op jit(solution)/shard_map/while/body/eval_jaxpr/slice | solution.py:87
  384.8 2.5 copy.70
  388.7 2.1 fusion.160
  390.8 2.5 copy.67
  393.3 2.5 copy.68
  404.2 84.1 %psum.7 = f32[4,1024]{1,0:T(4,128)S(1)} all-reduce(f32[4,1024]{1,0:T(4,128)S(1)} %bitcast.219), channel_id=1, replica_groups=mesh['ray'=16,'pix'=16] {'pix'}, use_global_device_ids=true, to_apply=%region_17.18 | all-reduce | flops 4096 | bytes 32768 | tf_op jit(solution)/shard_map/psum | solution.py:142
  (241 shorter events, 114.6 us)
Async XLA Ops:
  7.2 226.1 %reduce-scatter.4.cloned.1.call-start = ((), (), s32[]{:S(2)}) async-start(), calls=%async_computation.1 | async-start | bytes 1671168
  144.2 1.8 copy-start.6
  234.3 51.2 %copy-start.5 = (f32[64,384]{0,1:T(8,128)}, f32[64,384]{0,1:T(8,128)S(1)}, u32[]{:S(2)}) copy-start(f32[64,384]{0,1:T(8,128)S(1)} %copy.38) | copy-start | bytes 294916
  285.5 202.9 %copy-start.7 = (f32[2,1024]{1,0:T(2,128)S(1)}, f32[2,1024]{1,0:T(2,128)}, u32[]{:S(2)}) copy-start(f32[2,1024]{1,0:T(2,128)} %param.10) | copy-start | bytes 24580
  285.5 202.9 %copy-start.8 = (f32[2,1024]{1,0:T(2,128)S(1)}, f32[2,1024]{1,0:T(2,128)}, u32[]{:S(2)}) copy-start(f32[2,1024]{1,0:T(2,128)} %param.9) | copy-start | bytes 24580
  285.5 202.9 %copy-start.9 = (f32[1024]{0:T(1024)S(1)}, f32[1024]{0:T(1024)}, u32[]{:S(2)}) copy-start(f32[1024]{0:T(1024)} %param.12) | copy-start | bytes 12292
  306.8 1.8 copy-start.3
  306.8 2.3 copy-start.4
  311.4 1.4 copy-start
  311.4 1.5 copy-start.1
  311.4 1.8 copy-start.2
  336.5 1.8 copy-start.3
  336.5 2.3 copy-start.4
  341.1 1.4 copy-start
  341.1 1.5 copy-start.1
  341.1 1.8 copy-start.2
  366.2 1.8 copy-start.3
  366.2 2.3 copy-start.4
  370.8 1.4 copy-start
  370.8 1.5 copy-start.1
  370.8 1.8 copy-start.2
  395.9 1.8 copy-start.3
  395.9 2.3 copy-start.4
  400.4 1.4 copy-start
  400.4 1.5 copy-start.1
  400.5 1.8 copy-start.2
Sparse Core Ops, SparseCore 0:
  146.0 87.1 reduce-scatter.3
where the time goes:
time: 501 us; the launch traced here: 498 us
  blocking collectives  135 us (27%)
  other arithmetic  114 us (23%)
  local copies, waits for them, and re-layouts  98.7 us (20%)
  waiting for transfers between devices  87.3 us (17%)
  matrix products  44.4 us (9%)
  between operations  14.2 us (3%)
    unnamed x2, waiting for transfers between devices  87.3 us
    psum x1, blocking collectives, on_device(): sums = lax.psum(partial_value, 'pix')  84.1 us
    all_gather x1, blocking collectives, on_device(): gathered = lax.all_gather(grad_u, 'ray', axis=0, tiled=True)  51.1 us
    cos x1, other arithmetic, build_tables(): col_list.append(jnp.stack([jnp.cos(beta), jnp.sin(beta)]))  46.6 us
    dot_general x36, matrix products, product(): lax.dot_general(left, right, dims, preferred_element_type=jnp.float32)  44.4 us
    while x88, local copies, waits for them, and re-layouts  43.5 us
    slice x4, local copies, waits for them, and re-layouts, one_block(): b_re = b_blk[wave, 0]  20.6 us
    another operation x24, other arithmetic  16 us
  transfers between devices with their start and end apart: 1, of which 1 were waited for; matrix products, arithmetic and copies ran while one was open for 0% of the time, Pallas kernels for 0%

commit v1 on v0

--- a/solution.py
+++ b/solution.py
@@ -139,7 +139,7 @@
     psf, grad_u = intensity(field, psf_grad, clen, plen)
     gathered = lax.all_gather(grad_u, "ray", axis=0, tiled=True)
     partial_value = ray_partials(row_tab, col_tab, rows_x, all_cols, gathered)
-    sums = lax.psum(partial_value, "pix")
+    sums = jnp.sum(lax.all_gather(partial_value, "pix"), axis=0)
     return (psf, finish(sums, rays))
 
 

time: 501 us -> 451 us (0.900); the launches traced: 498 us -> 443 us
  blocking collectives: 135 us -> 80 us
    psum x1 -> x0, blocking collectives: 84.1 us -> none  [on_device(): sums = lax.psum(partial_value, 'pix')]
    all_gather x0 -> x1, blocking collectives: none -> 29 us  [on_device(): sums = jnp.sum(lax.all_gather(partial_value, 'pix'), axis=0)]
where the time goes in v1:
time: 451 us; the launch traced here: 443 us
  other arithmetic  114 us (25%)
  local copies, waits for them, and re-layouts  98.7 us (22%)
  waiting for transfers between devices  87.3 us (19%)
  blocking collectives  80 us (18%)
  matrix products  44.4 us (10%)
  between operations  14.2 us (3%)
    unnamed x2, waiting for transfers between devices  87.3 us
    all_gather x1, blocking collectives, on_device(): gathered = lax.all_gather(grad_u, 'ray', axis=0, tiled=True)  51.1 us
    cos x1, other arithmetic, build_tables(): col_list.append(jnp.stack([jnp.cos(beta), jnp.sin(beta)]))  46.6 us
    dot_general x36, matrix products, product(): lax.dot_general(left, right, dims, preferred_element_type=jnp.float32)  44.4 us
    while x88, local copies, waits for them, and re-layouts  43.5 us
    all_gather x1, blocking collectives, on_device(): sums = jnp.sum(lax.all_gather(partial_value, 'pix'), axis=0)  29 us
    slice x4, local copies, waits for them, and re-layouts, one_block(): b_re = b_blk[wave, 0]  20.6 us
    another operation x24, other arithmetic  16 us
  transfers between devices with their start and end apart: 1, of which 1 were waited for; matrix products, arithmetic and copies ran while one was open for 0% of the time, Pallas kernels for 0%

profile of v1, /device:TPU:32, one launch (start us, length us, event | category | flops | bytes accessed | tf_op | source)
XLA Modules:
  0.0 442.7 jit_solution(11877989996729009138)
XLA Ops:
  9.5 3.6 cosine_multiply_fusion.2
  13.2 46.6 %multiply_cosine_fusion.2 = (f32[1,1024,1024]{2,1,0:T(8,128)}, f32[1,1024,1024]{2,1,0:T(8,128)}, f32[1,1024,1024]{2,1,0:T(8,128)}, f32[1,1024,1024]{2,1,0:T(8,12...) fusion(f32[1024]{0:T(1024)S(1)} %bitcast.214, f32[1024]{0:T(1024)S(1)} %fusion.111, ...), kind=kLoop, calls=%fused_computation.186 | loop fusion | flops 3145728 | bytes 25182208 | tf_op jit(solution)/shard_map/cos | solution.py:32
  62.8 9.3 %maximum_bitcast_fusion.1 = (f32[1,2,1024,1024]{3,2,1,0:T(8,128)S(1)}, f32[1,2,1024,1024]{3,2,1,0:T(8,128)}) fusion(f32[1,1024,1024]{2,1,0:T(8,128)} %get-tuple-element.336, f32[1,1024,1024]{2,1,0:T(8,128)} %get-tuple-element.335, f32[1,1024,1024]{2,1,0:T(8,128)} %get-tuple-element.341, f32[1,1024,1024]{2,1,0:T(8,128)} %get-tuple-element.342), kind=kLoop, calls=%fused_computation.178 | loop fusion | flops 4194304 | bytes 33554432 | tf_op jit(solution)/shard_map/stack | solution.py:33
  72.1 15.7 %fusion.115 = (bf16[3,2,1024,1024]{3,2,1,0:T(8,128)(2,1)}, f32[3,2,1024,1024]{3,2,1,0:T(8,128)}) fusion(f32[1,2,1024,1024]{3,2,1,0:T(8,128)S(1)} %maximum_bitcast_fusion.3, f32[1,2,1024,1024]{3,2,1,0:T(8,128)} %get-tuple-element.346, f32[1,2,1024,1024]{3,2,1,0:T(8,128)S(1)} %get-tuple-element.345), kind=kLoop, calls=%fused_computation.219 | loop fusion | flops 18874368 | bytes 62914560
  87.8 56.3 %while.27 = (s32[]{:T(128)}, f32[1024,384]{0,1:T(8,128)S(1)}, bf16[3,2,1024,1024]{3,2,1,0:T(8,128)(2,1)}, f32[3,2,1024,64]{2,3,1,0:T(8,128)}, s32[]{:T(128)}, /*...) while((s32[]{:T(128)}, f32[1024,384]{0,1:T(8,128)S(1)}, bf16[3,2,1024,1024]{3,2,1,0:T(8,128)(2,1)}, ...), condition=%wide.region_1.0_spmd.clone, body=%wide.region_0.0_spmd.clone.sunk | while | flops 412237824 | bytes 23888080 | solution.py:67
  96.0 2.5 fusion.173
  110.1 2.5 fusion.173
  124.2 2.5 fusion.173
  138.2 2.5 fusion.173
  145.9 87.3 %reduce-scatter.4.cloned.1.call-done = f32[64,384]{1,0:T(8,128)} async-done(((f32[1024,384]{1,0:T(8,128)}), f32[64,384]{1,0:T(8,128)}) %reduce-scatter.4.cloned.1.call-update) | async-done | bytes 98320
  234.4 51.1 %all_gather.6 = bf16[1024,384]{1,0:T(8,128)(2,1)} all-gather(bf16[64,384]{1,0:T(8,128)(2,1)S(1)} %copy.31), channel_id=1, replica_groups=mesh['ray'=16,'pix'=16] {'ray'}, dimensions={0}, use_global_device_ids=true | all-gather | bytes 835584 | tf_op jit(solution)/shard_map/all_gather | solution.py:140
  285.5 118.7 %while.26 = (s32[]{:T(128)}, f32[4,4,256]{2,1,0:T(4,128)S(1)}, s32[4]{0:T(128)S(1)}, f32[3,2,1024,1024]{3,2,1,0:T(8,128)}, bf16[1024,384]{1,0:T(8,128)(2,1)}, /*...) while((s32[]{:T(128)}, f32[4,4,256]{2,1,0:T(4,128)S(1)}, ...), condition=%wide.region_16.17_spmd.clone.clone, body=%wide.region_3.16_spmd.clone.clone.sunk | while | flops 819468480 | bytes 79344528 | solution.py:104
  286.7 5.2 %constant_dynamic-slice_fusion.15 = (f32[1,1,1024,256]{3,2,1,0:T(8,128)S(1)}, f32[1,1,1024,256]{3,2,1,0:T(8,128)}, f32[1,1,1024,256]{3,2,1,0:T(8,128)}, f32[1,1,...) fusion(f32[3,2,1024,1024]{3,2,1,0:T(8,128)} %get-tuple-element.584, ...), kind=kLoop, calls=%fused_computation.102.clone.1 | loop fusion | bytes 12582924 | tf_op jit(solution)/shard_map/while/body/eval_jaxpr/slice | solution.py:87
  295.7 2.5 copy.70
  301.8 2.5 copy.67
  304.3 2.5 copy.68
  316.4 5.2 %constant_dynamic-slice_fusion.15 = (f32[1,1,1024,256]{3,2,1,0:T(8,128)S(1)}, f32[1,1,1024,256]{3,2,1,0:T(8,128)}, f32[1,1,1024,256]{3,2,1,0:T(8,128)}, f32[1,1,...) fusion(f32[3,2,1024,1024]{3,2,1,0:T(8,128)} %get-tuple-element.584, ...), kind=kLoop, calls=%fused_computation.102.clone.1 | loop fusion | bytes 12582924 | tf_op jit(solution)/shard_map/while/body/eval_jaxpr/slice | solution.py:87
  325.4 2.5 copy.70
  329.3 2.1 fusion.160
  331.5 2.5 copy.67
  334.0 2.5 copy.68
  346.1 5.2 %constant_dynamic-slice_fusion.15 = (f32[1,1,1024,256]{3,2,1,0:T(8,128)S(1)}, f32[1,1,1024,256]{3,2,1,0:T(8,128)}, f32[1,1,1024,256]{3,2,1,0:T(8,128)}, f32[1,1,...) fusion(f32[3,2,1024,1024]{3,2,1,0:T(8,128)} %get-tuple-element.584, ...), kind=kLoop, calls=%fused_computation.102.clone.1 | loop fusion | bytes 12582924 | tf_op jit(solution)/shard_map/while/body/eval_jaxpr/slice | solution.py:87
  355.1 2.5 copy.70
  359.0 2.1 fusion.160
  361.1 2.5 copy.67
  363.7 2.5 copy.68
  375.8 5.2 %constant_dynamic-slice_fusion.15 = (f32[1,1,1024,256]{3,2,1,0:T(8,128)S(1)}, f32[1,1,1024,256]{3,2,1,0:T(8,128)}, f32[1,1,1024,256]{3,2,1,0:T(8,128)}, f32[1,1,...) fusion(f32[3,2,1024,1024]{3,2,1,0:T(8,128)} %get-tuple-element.584, ...), kind=kLoop, calls=%fused_computation.102.clone.1 | loop fusion | bytes 12582924 | tf_op jit(solution)/shard_map/while/body/eval_jaxpr/slice | solution.py:87
  384.8 2.5 copy.70
  388.7 2.1 fusion.160
  390.8 2.5 copy.67
  393.3 2.5 copy.68
  404.2 29.0 %all_gather.7 = f32[16,4,1024]{2,1,0:T(4,128)S(1)} all-gather(f32[1,4,1024]{2,1,0:T(4,128)S(1)} %bitcast.219), channel_id=1, replica_groups=mesh['ray'=16,'pix'=16] {'pix'}, dimensions={0}, use_global_device_ids=true | all-gather | bytes 278528 | tf_op jit(solution)/shard_map/all_gather | solution.py:142
  (242 shorter events, 114.7 us)
Async XLA Ops:
  7.2 226.1 %reduce-scatter.4.cloned.1.call-start = ((), (), s32[]{:S(2)}) async-start(), calls=%async_computation.1 | async-start | bytes 1671168
  144.2 1.8 copy-start.6
  234.3 51.2 %copy-start.5 = (f32[64,384]{0,1:T(8,128)}, f32[64,384]{0,1:T(8,128)S(1)}, u32[]{:S(2)}) copy-start(f32[64,384]{0,1:T(8,128)S(1)} %copy.38) | copy-start | bytes 294916
  285.5 147.8 %copy-start.7 = (f32[2,1024]{1,0:T(2,128)S(1)}, f32[2,1024]{1,0:T(2,128)}, u32[]{:S(2)}) copy-start(f32[2,1024]{1,0:T(2,128)} %param.10) | copy-start | bytes 24580
  285.5 147.8 %copy-start.8 = (f32[2,1024]{1,0:T(2,128)S(1)}, f32[2,1024]{1,0:T(2,128)}, u32[]{:S(2)}) copy-start(f32[2,1024]{1,0:T(2,128)} %param.9) | copy-start | bytes 24580
  285.5 147.8 %copy-start.9 = (f32[1024]{0:T(1024)S(1)}, f32[1024]{0:T(1024)}, u32[]{:S(2)}) copy-start(f32[1024]{0:T(1024)} %param.12) | copy-start | bytes 12292
  306.8 1.8 copy-start.3
  306.8 2.3 copy-start.4
  311.4 1.4 copy-start
  311.4 1.5 copy-start.1
  311.4 1.8 copy-start.2
  336.5 1.8 copy-start.3
  336.5 2.3 copy-start.4
  341.1 1.4 copy-start
  341.1 1.5 copy-start.1
  341.1 1.8 copy-start.2
  366.2 1.8 copy-start.3
  366.2 2.3 copy-start.4
  370.8 1.4 copy-start
  370.8 1.5 copy-start.1
  370.8 1.8 copy-start.2
  395.9 1.8 copy-start.3
  395.9 2.3 copy-start.4
  400.4 1.4 copy-start
  400.4 1.5 copy-start.1
  400.5 1.8 copy-start.2
Sparse Core Ops, SparseCore 0:
  146.0 87.1 reduce-scatter.3
